TPU v7x, 128 devices: a whole 4x4x4 slice. The times are simulated.
128 devices in a mesh: dp: 2 (over z_lo), head: 8 (over z_hi, y), tensor: 8 (over x, core).
Axes of the slice: x: 4, y: 4, z: 4 (z_hi: 2, z_lo: 2; z = z_hi * 2 + z_lo), core: 2. Of those that a mesh axis runs over, the one named last changes fastest.
Arguments:
- tokens: bfloat16 [512, 8192], P('dp', 'tensor'), may hold values from -6 to 6
- cotangent: bfloat16 [512, 8192], P('dp', 'tensor'), may hold values from -6 to 6
- w_gate: bfloat16 [8192, 29568], P('tensor', 'head'), may hold values from -0.0625 to 0.0625
- w_up: bfloat16 [8192, 29568], P('tensor', 'head'), may hold values from -0.0625 to 0.0625
- w_down: bfloat16 [29568, 8192], P('head', 'tensor'), may hold values from -0.03125 to 0.03125
- common_down_factor: bfloat16 [8192, 64], P('tensor'), may hold values from -0.0625 to 0.0625
- head_up: bfloat16 [64, 64, 8192], P('head', None, 'tensor'), may hold values from -0.0625 to 0.0625
- routes: int32 [512, 1], P('dp'), may hold values from 0 to 63
Outputs:
- grad_x: bfloat16 [512, 8192], P(('dp', 'head'), 'tensor')
- grad_shared: float32 [8192, 64], P('tensor')
- up_head_gradients: float32 [64, 64, 8192], P('head', None, 'tensor')
Inputs may be any that keep to these rules, and one draw needn't show every extreme that they name: `routes`: each token names one adapter head; the loads are skewed.
All inputs are finite; a program needn't handle non-finite values.
Results may differ from a plain program's by a relative error of at most 0.015.
Values may be sent and summed in bfloat16 or wider, within the bound.
A program may use at most 128 MiB of HBM per device.

v0:
```python
import jax
import jax.numpy as jnp
from jax import lax
from jax.sharding import PartitionSpec as P

ADAPTER_SCALE = 2.0


def contract_last(left, right):
    return lax.dot_general(
        left, right, (((1,), (1,)), ((), ())), preferred_element_type=jnp.float32
    )


def local(tokens, cotangent, w_gate, w_up, w_down, common_down_factor, head_up, routes):
    tok_rows, d_cols = tokens.shape
    hidden_activation = w_gate.shape[1]
    reduced_activation = common_down_factor.shape[1]
    local_heads = head_up.shape[0]
    first_head = lax.axis_index("head") * local_heads
    assigned_mask = (
        routes == first_head + jnp.arange(local_heads, dtype=jnp.int32)[None, :]
    ).astype(jnp.float32)
    flat_heads = head_up.reshape(local_heads * reduced_activation, d_cols)
    gate_preactivation = jnp.dot(tokens, w_gate, preferred_element_type=jnp.float32)
    up_preactivation = jnp.dot(tokens, w_up, preferred_element_type=jnp.float32)
    returned_gradient = contract_last(cotangent, w_down)
    adapter_selectors = jnp.dot(tokens, common_down_factor, preferred_element_type=jnp.float32)
    head_separated = contract_last(cotangent, flat_heads).reshape(
        tok_rows, local_heads, reduced_activation
    )
    selector_gradient = ADAPTER_SCALE * jnp.sum(head_separated * assigned_mask[:, :, None], axis=1)
    partial = jnp.concatenate(
        [
            gate_preactivation.astype(jnp.bfloat16),
            up_preactivation.astype(jnp.bfloat16),
            returned_gradient.astype(jnp.bfloat16),
            adapter_selectors.astype(jnp.bfloat16),
            selector_gradient.astype(jnp.bfloat16),
        ],
        axis=1,
    )
    own_rows = lax.psum_scatter(partial, "tensor", scatter_dimension=0, tiled=True)
    gate_preactivation = own_rows[:, :hidden_activation].astype(jnp.float32)
    up_preactivation = own_rows[:, hidden_activation : 2 * hidden_activation].astype(jnp.float32)
    returned_gradient = own_rows[:, 2 * hidden_activation : 3 * hidden_activation].astype(
        jnp.float32
    )
    sig_gate = jax.nn.sigmoid(gate_preactivation)
    gate_gradient = (
        returned_gradient
        * up_preactivation
        * sig_gate
        * (1.0 + gate_preactivation * (1.0 - sig_gate))
    ).astype(jnp.bfloat16)
    up_gradient = (returned_gradient * gate_preactivation * sig_gate).astype(jnp.bfloat16)
    gathered = lax.all_gather(
        jnp.concatenate([gate_gradient, up_gradient, own_rows[:, 3 * hidden_activation :]], axis=1),
        "tensor",
        axis=0,
        tiled=True,
    )
    gate_gradient = gathered[:, :hidden_activation]
    up_gradient = gathered[:, hidden_activation : 2 * hidden_activation]
    adapter_selectors = gathered[
        :, 2 * hidden_activation : 2 * hidden_activation + reduced_activation
    ]
    selector_gradient = gathered[:, 2 * hidden_activation + reduced_activation :]
    ffn_part = (
        contract_last(gate_gradient, w_gate)
        + contract_last(up_gradient, w_up)
        + contract_last(selector_gradient, common_down_factor)
    )
    grad_x = lax.psum_scatter(
        ffn_part.astype(jnp.bfloat16), "head", scatter_dimension=0, tiled=True
    )
    selector_mask = (
        adapter_selectors[:, None, :] * assigned_mask[:, :, None].astype(jnp.bfloat16)
    ).reshape(tok_rows, local_heads * reduced_activation)
    head_contributions = ADAPTER_SCALE * lax.dot_general(
        selector_mask, cotangent, (((0,), (0,)), ((), ())), preferred_element_type=jnp.float32
    )
    up_head_gradients = lax.psum(
        head_contributions.reshape(local_heads, reduced_activation, d_cols).astype(jnp.bfloat16),
        "dp",
    ).astype(jnp.float32)
    shared_term = lax.dot_general(
        tokens, selector_gradient, (((0,), (0,)), ((), ())), preferred_element_type=jnp.float32
    )
    grad_shared = lax.psum(shared_term.astype(jnp.bfloat16), ("dp", "head")).astype(jnp.float32)
    return (grad_x, grad_shared, up_head_gradients)


def solution(mesh):
    placed = (
        P("dp", "tensor"),
        P("dp", "tensor"),
        P("tensor", "head"),
        P("tensor", "head"),
        P("head", "tensor"),
        P("tensor", None),
        P("head", None, "tensor"),
        P("dp", None),
    )
    return jax.shard_map(
        local,
        mesh=mesh,
        in_specs=placed,
        out_specs=(P(("dp", "head"), "tensor"), P("tensor", None), P("head", None, "tensor")),
        check_vma=False,
    )
```

profile of v0, /device:TPU:0, one launch (start us, length us, event | category | flops | bytes accessed | tf_op | source)
XLA Modules:
  0.0 327.6 jit_solution(7032396311072623166)
XLA Ops:
  7.2 0.8 fusion.27
  8.1 6.9 %fusion.2 = bf16[256,11216]{0,1:T(8,128)(2,1)} fusion(bf16[256,1024]{1,0:T(8,128)(2,1)} %param.8, bf16[1024,3696]{0,1:T(8,128)(2,1)} %param.10), kind=kOutput, calls=%fused_computation.5 | convolution fusion | flops 1938714624 | bytes 9986048 | tf_op jit(solution)/shard_map/dot_general | solution.py:25
  15.0 3.5 %fusion.1 = bf16[256,11216]{0,1:T(8,128)(2,1)} fusion(bf16[256,11216]{0,1:T(8,128)(2,1)} %fusion.2, bf16[256,1024]{1,0:T(8,128)(2,1)S(1)} %copy-done.1, bf16[1024,3696]{0,1:T(8,128)(2,1)S(1)} %copy-done.5), kind=kOutput, calls=%fused_computation.3 | convolution fusion | flops 1938714624 | bytes 9986048 | tf_op jit(solution)/shard_map/dot_general | solution.py:26
  18.5 0.5 fusion.11
  19.0 3.4 %fusion = bf16[256,11216]{0,1:T(8,128)(2,1)} fusion(bf16[256,11216]{0,1:T(8,128)(2,1)} %fusion.1, bf16[256,1024]{1,0:T(8,128)(2,1)S(1)} %copy-done.2, bf16[3696,1024]{1,0:T(8,128)(2,1)S(1)} %bitcast.28), kind=kOutput, calls=%fused_computation.1 | convolution fusion | flops 1938714624 | bytes 9986048 | tf_op jit(solution)/shard_map/dot_general | solution.py:10
  22.5 0.9 fusion.13
  23.4 0.6 fusion.26
  24.0 8.5 %copy.22 = bf16[256,11216]{1,0:T(8,128)(2,1)} copy(bf16[256,11216]{0,1:T(8,128)(2,1)} %fusion.26) | data formatting | bytes 11485184
  32.5 43.7 %reduce-scatter.7.cloned.1.call-done = bf16[32,11216]{1,0:T(8,128)(2,1)} async-done(((bf16[256,11216]{1,0:T(8,128)(2,1)}), bf16[32,11216]{1,0:T(8,128)(2,1)}) %reduce-scatter.7.cloned.1.call-update) | async-done | bytes 717840 | tf_op jit(solution)/shard_map/reduce_scatter | solution.py:43
  76.2 0.8 slice.35
  77.0 1.5 fusion.23
  78.6 1.0 concatenate.7
  79.7 30.3 %all-gather.2.cloned.1.call-done = bf16[256,7520]{1,0:T(8,128)(2,1)} async-done(((bf16[32,7520]{1,0:T(8,128)(2,1)}), bf16[256,7520]{1,0:T(8,128)(2,1)}) %all-gather.2.cloned.1.call-update) | async-done | bytes 3850256 | tf_op jit(solution)/shard_map/all_gather | solution.py:57
  110.0 1.0 slice.39
  111.1 1.8 fusion.12
  113.0 1.4 multiply_convert_fusion
  114.7 6.1 %fusion.3 = f32[256,1024]{1,0:T(8,128)S(1)} fusion(bf16[1024,3696]{0,1:T(8,128)(2,1)} %param.11, bf16[256,7520]{1,0:T(8,128)(2,1)} %all-gather.2.cloned.1.call-done), kind=kOutput, calls=%fused_computation.7 | convolution fusion | flops 1937768448 | bytes 10518528 | tf_op jit(solution)/shard_map/dot_general | solution.py:10
  120.8 5.5 %fusion.7 = f32[256,1024]{1,0:T(8,128)S(1)} fusion(f32[256,1024]{1,0:T(8,128)S(1)} %fusion.3, bf16[1024,3696]{0,1:T(8,128)(2,1)} %param.10, bf16[256,7520]{1,0:T(8,128)(2,1)S(1)} %copy-done.4), kind=kOutput, calls=%fused_computation.12 | convolution fusion | flops 1938030592 | bytes 11567104 | tf_op jit(solution)/shard_map/dot_general | solution.py:10
  126.3 1.1 fusion.10
  127.5 68.6 %all-reduce.3.cloned.1.call-done = bf16[1024,64]{0,1:T(8,128)(2,1)} async-done(((bf16[1024,64]{0,1:T(8,128)(2,1)}), bf16[1024,64]{0,1:T(8,128)(2,1)}) %all-reduce.3.cloned.1.call-update) | async-done | bytes 131088 | tf_op jit(solution)/shard_map/psum | solution.py:90
  196.1 1.6 convert_element_type.83
  197.8 47.5 %all-reduce.5.cloned.1.call-done = bf16[8,64,1024]{2,1,0:T(8,128)(2,1)} async-done(((bf16[8,64,1024]{2,1,0:T(8,128)(2,1)}), bf16[8,64,1024]{2,1,0:T(8,128)(2,1)}) %all-reduce.5.cloned.1.call-update) | async-done | bytes 1048592 | tf_op jit(solution)/shard_map/psum | solution.py:83
  245.2 2.8 convert_element_type.87
  248.0 73.1 %reduce-scatter.5.cloned.1.call-done = bf16[32,1024]{1,0:T(8,128)(2,1)} async-done(((bf16[256,1024]{1,0:T(8,128)(2,1)}), bf16[32,1024]{1,0:T(8,128)(2,1)}) %reduce-scatter.5.cloned.1.call-update) | async-done | bytes 65552 | tf_op jit(solution)/shard_map/reduce_scatter | solution.py:74
  (30 shorter events, 0.6 us)
Async XLA Ops:
  7.2 11.3 %copy-start = (bf16[8,64,1024]{2,1,0:T(8,128)(2,1)S(1)}, bf16[8,64,1024]{2,1,0:T(8,128)(2,1)}, u32[]{:S(2)}) copy-start(bf16[8,64,1024]{2,1,0:T(8,128)(2,1)} %param.14) | copy-start | bytes 3145732
  7.2 69.1 %reduce-scatter.7.cloned.1.call-start = ((), (), s32[]{:S(2)}) async-start(), calls=%async_computation.6 | async-start | bytes 6488064 | tf_op jit(solution)/shard_map/reduce_scatter | solution.py:43
  8.1 6.9 %copy-start.1 = (bf16[256,1024]{1,0:T(8,128)(2,1)S(1)}, bf16[256,1024]{1,0:T(8,128)(2,1)}, u32[]{:S(2)}) copy-start(bf16[256,1024]{1,0:T(8,128)(2,1)} %param.8) | copy-start | bytes 1572868
  8.1 6.9 %copy-start.5 = (bf16[1024,3696]{0,1:T(8,128)(2,1)S(1)}, bf16[1024,3696]{0,1:T(8,128)(2,1)}, u32[]{:S(2)}) copy-start(bf16[1024,3696]{0,1:T(8,128)(2,1)} %param.11) | copy-start | bytes 22708228
  8.1 10.9 %slice-start = ((s8[7569408]{0:T(1024)(128)(4,1)}), s8[4194304]{0:T(1024)(128)(4,1)S(1)}, s32[]{:S(2)}) async-start(s8[7569408]{0:T(1024)(128)(4,1)} %bitcast.27), calls=%async_computation.7 | async-start | bytes 8388608
  15.0 3.5 %copy-start.2 = (bf16[256,1024]{1,0:T(8,128)(2,1)S(1)}, bf16[256,1024]{1,0:T(8,128)(2,1)}, u32[]{:S(2)}) copy-start(bf16[256,1024]{1,0:T(8,128)(2,1)} %param.9) | copy-start | bytes 1572868
  15.0 4.0 %slice-start.1 = ((s8[7569408]{0:T(1024)(128)(4,1)}), s8[3375104]{0:T(1024)(128)(4,1)S(1)}, s32[]{:S(2)}) async-start(s8[7569408]{0:T(1024)(128)(4,1)} %bitcast.27), calls=%async_computation.8 | async-start | bytes 6750208
  19.0 3.5 %copy-start.3 = (bf16[1024,64]{0,1:T(8,128)(2,1)S(1)}, bf16[1024,64]{0,1:T(8,128)(2,1)}, u32[]{:S(2)}) copy-start(bf16[1024,64]{0,1:T(8,128)(2,1)} %param.13) | copy-start | bytes 393220
  32.5 77.5 %all-gather.2.cloned.1.call-start = ((), (), s32[]{:S(2)}) async-start(), calls=%async_computation.2 | async-start | bytes 4349952 | tf_op jit(solution)/shard_map/all_gather | solution.py:57
  79.6 116.5 %all-reduce.3.cloned.1.call-start = ((), (), s32[]{:S(2)}) async-start(), calls=%async_computation.4 | async-start | bytes 262144 | tf_op jit(solution)/shard_map/psum | solution.py:90
  112.9 132.3 %all-reduce.5.cloned.1.call-start = ((), (), s32[]{:S(2)}) async-start(), calls=%async_computation.5 | async-start | bytes 2097152 | tf_op jit(solution)/shard_map/psum | solution.py:83
  114.4 206.7 %reduce-scatter.5.cloned.1.call-start = ((), (), s32[]{:S(2)}) async-start(), calls=%async_computation.3 | async-start | bytes 589824 | tf_op jit(solution)/shard_map/reduce_scatter | solution.py:74
  114.7 6.1 %copy-start.4 = (bf16[256,7520]{1,0:T(8,128)(2,1)S(1)}, bf16[256,7520]{1,0:T(8,128)(2,1)}, u32[]{:S(2)}) copy-start(bf16[256,7520]{1,0:T(8,128)(2,1)} %all-gather.2.cloned.1.call-done) | copy-start | bytes 11550724
Sparse Core Ops, SparseCore 0:
  32.6 43.6 reduce-scatter.6
  79.7 30.2 all-gather.1
  113.8 82.3 all-reduce.2
  199.2 46.0 all-reduce.4
  249.2 71.8 reduce-scatter.4
where the time goes:
time: 328 us
  waiting for transfers between devices  263 us (80%)
  matrix products  31.2 us (10%)
  between operations  13.9 us (4%)
  local copies, waits for them, and re-layouts  11.4 us (3%)
  other arithmetic  7.4 us (2%)
    reduce_scatter x1, waiting for transfers between devices, local(): lax.psum_scatter(ffn_part.astype(jnp.bfloat16), 'head', scatter_dimension...  73.1 us
    psum x1, waiting for transfers between devices, local(): lax.psum(shared_term.astype(jnp.bfloat16), ('dp', 'head'))  68.6 us
    psum x1, waiting for transfers between devices, local(): lax.psum(head_contributions.reshape(local_heads, reduced_activation, d_co...  47.5 us
    reduce_scatter x1, waiting for transfers between devices, local(): lax.psum_scatter(partial, 'tensor', scatter_dimension=0, tiled=True)  43.7 us
    all_gather x1, waiting for transfers between devices, local(): lax.all_gather(jnp.concatenate([gate_gradient, up_gradient, own_rows[:, 3...  30.3 us
    dot_general x5, matrix products, contract_last(): lax.dot_general(left, right, (((1,), (1,)), ((), ())), preferred_element_...  16.7 us
    unnamed x17, local copies, waits for them, and re-layouts  8.5 us
    dot_general x1, matrix products, local(): jnp.dot(tokens, w_gate, preferred_element_type=jnp.float32)  6.88 us
  transfers between devices with their start and end apart: 5, of which 5 were waited for; matrix products, arithmetic and copies ran while one was open for 6% of the time, Pallas kernels for 0%

commit v1 on v0

--- a/solution.py
+++ b/solution.py
@@ -4,6 +4,28 @@
 from jax.sharding import PartitionSpec as P
 
 ADAPTER_SCALE = 2.0
+
+
+def laid_out(blocks, dim):
+    blocks = jnp.moveaxis(blocks, 0, dim)
+    shape = blocks.shape
+    return blocks.reshape(*shape[:dim], shape[dim] * shape[dim + 1], *shape[dim + 2 :])
+
+
+def collect(x, axis, dim):
+    size = lax.axis_size(axis)
+    pairs = [(i, (i + 1) % size) for i in range(size)]
+    back = [(b, a) for a, b in pairs]
+    lower, upper = ([], [])
+    for turn in range(size - 1):
+        if turn % 2 == 0:
+            lower.append(lax.ppermute(lower[-1] if lower else x, axis, pairs))
+        else:
+            upper.append(lax.ppermute(upper[-1] if upper else x, axis, back))
+    blocks = jnp.stack([*lower[::-1], x, *upper])
+    shift = lax.axis_index(axis) - len(lower)
+    blocks = blocks[(jnp.arange(size) - shift) % size]
+    return laid_out(blocks, dim)
 
 
 def contract_last(left, right):
@@ -54,11 +76,10 @@
         * (1.0 + gate_preactivation * (1.0 - sig_gate))
     ).astype(jnp.bfloat16)
     up_gradient = (returned_gradient * gate_preactivation * sig_gate).astype(jnp.bfloat16)
-    gathered = lax.all_gather(
+    gathered = collect(
         jnp.concatenate([gate_gradient, up_gradient, own_rows[:, 3 * hidden_activation :]], axis=1),
         "tensor",
-        axis=0,
-        tiled=True,
+        0,
     )
     gate_gradient = gathered[:, :hidden_activation]
     up_gradient = gathered[:, hidden_activation : 2 * hidden_activation]

time: 328 us -> 350 us (1.067)
  local copies, waits for them, and re-layouts: 11.4 us -> 27.9 us
  starting transfers between devices: 0.39 us -> 8.73 us
    all_gather x1 -> x0, waiting for transfers between devices: 30.3 us -> none  [local(): lax.all_gather(jnp.concatenate([gate_gradient, up_gradient, own_rows[:, 3...]
    ppermute x0 -> x7, waiting for transfers between devices: none -> 28.8 us  [the longest x4 28.6 us: collect(): lower.append(lax.ppermute(lower[-1] if lower else x, axis, pairs))]
    unnamed x17 -> x26, local copies, waits for them, and re-layouts: 8.5 us -> 20 us
    ppermute x0 -> x7, starting transfers between devices: none -> 8.38 us  [the longest x3 8.36 us: collect(): upper.append(lax.ppermute(upper[-1] if upper else x, axis, back))]
    gather x0 -> x1, local copies, waits for them, and re-layouts: none -> 4.87 us  [collect(): blocks = blocks[(jnp.arange(size) - shift) % size]]
  transfers between devices with their start and end apart: 5 -> 11, of which waited for: 5 -> 9; matrix products, arithmetic and copies ran while one was open for 6% -> 8% of each run, Pallas kernels for 0% -> 0%
where the time goes in v1:
time: 350 us; the launch traced here: 349 us
  waiting for transfers between devices  260 us (74%)
  matrix products  31.2 us (9%)
  local copies, waits for them, and re-layouts  27.9 us (8%)
  between operations  13.9 us (4%)
  starting transfers between devices  8.73 us (2%)
  other arithmetic  7.42 us (2%)
    reduce_scatter x1, waiting for transfers between devices, local(): lax.psum_scatter(ffn_part.astype(jnp.bfloat16), 'head', scatter_dimension...  73.1 us
    psum x1, waiting for transfers between devices, local(): lax.psum(shared_term.astype(jnp.bfloat16), ('dp', 'head'))  66.7 us
    psum x1, waiting for transfers between devices, local(): lax.psum(head_contributions.reshape(local_heads, reduced_activation, d_co...  47.6 us
    reduce_scatter x1, waiting for transfers between devices, local(): lax.psum_scatter(partial, 'tensor', scatter_dimension=0, tiled=True)  43.7 us
    ppermute x4, waiting for transfers between devices, collect(): lower.append(lax.ppermute(lower[-1] if lower else x, axis, pairs))  28.6 us
    unnamed x26, local copies, waits for them, and re-layouts  20 us
    dot_general x5, matrix products, contract_last(): lax.dot_general(left, right, (((1,), (1,)), ((), ())), preferred_element_...  16.7 us
    ppermute x3, starting transfers between devices, collect(): upper.append(lax.ppermute(upper[-1] if upper else x, axis, back))  8.36 us
  transfers between devices with their start and end apart: 11, of which 9 were waited for; matrix products, arithmetic and copies ran while one was open for 8% of the time, Pallas kernels for 0%

profile of v1, /device:TPU:0, one launch (start us, length us, event | category | flops | bytes accessed | tf_op | source)
XLA Modules:
  0.0 349.1 jit_solution(14138412070372311462)
XLA Ops:
  8.1 6.9 %fusion.2 = bf16[256,11216]{0,1:T(8,128)(2,1)} fusion(bf16[256,1024]{1,0:T(8,128)(2,1)} %param.8, bf16[1024,3696]{0,1:T(8,128)(2,1)} %param.10), kind=kOutput, calls=%fused_computation.6 | convolution fusion | flops 1938714624 | bytes 9986048 | tf_op jit(solution)/shard_map/dot_general | solution.py:47
  15.0 3.5 %fusion.1 = bf16[256,11216]{0,1:T(8,128)(2,1)} fusion(bf16[256,11216]{0,1:T(8,128)(2,1)} %fusion.2, bf16[256,1024]{1,0:T(8,128)(2,1)S(1)} %copy-done.2, bf16[1024,3696]{0,1:T(8,128)(2,1)S(1)} %copy-done.6), kind=kOutput, calls=%fused_computation.4 | convolution fusion | flops 1938714624 | bytes 9986048 | tf_op jit(solution)/shard_map/dot_general | solution.py:48
  19.0 3.4 fusion
  23.9 8.4 %copy.23 = bf16[256,11216]{1,0:T(8,128)(2,1)} copy(bf16[256,11216]{0,1:T(8,128)(2,1)} %fusion.26) | data formatting | bytes 11485184
  32.4 43.7 %reduce-scatter.7.cloned.1.call-done = bf16[32,11216]{1,0:T(8,128)(2,1)} async-done(((bf16[256,11216]{1,0:T(8,128)(2,1)}), bf16[32,11216]{1,0:T(8,128)(2,1)}) %reduce-scatter.7.cloned.1.call-update) | async-done | bytes 717840 | tf_op jit(solution)/shard_map/reduce_scatter | solution.py:65
  78.7 9.4 %collective-permute-done = bf16[32,7520]{1,0:T(8,128)(2,1)S(1)} collective-permute-done((bf16[32,7520]{1,0:T(8,128)(2,1)S(1)}, bf16[32,7520]{1,0:T(8,128)(2,1)S(1)}, u32[]{:S(2)}, u32[]{:S(2)}) %collective-permute-start) | collective-permute-done | bytes 481312 | tf_op jit(solution)/shard_map/ppermute | solution.py:22
  88.1 3.0 collective-permute-start.4
  91.0 6.4 %collective-permute-done.1 = bf16[32,7520]{1,0:T(8,128)(2,1)S(1)} collective-permute-done((bf16[32,7520]{1,0:T(8,128)(2,1)S(1)}, bf16[32,7520]{1,0:T(8,128)(2,1)S(1)}, u32[]{:S(2)}, u32[]{:S(2)}) %collective-permute-start.1) | collective-permute-done | bytes 481312 | tf_op jit(solution)/shard_map/ppermute | solution.py:22
  98.2 2.3 collective-permute-start.5
  100.5 6.4 %collective-permute-done.2 = bf16[32,7520]{1,0:T(8,128)(2,1)} collective-permute-done((bf16[32,7520]{1,0:T(8,128)(2,1)S(1)}, bf16[32,7520]{1,0:T(8,128)(2,1)}, u32[]{:S(2)}, u32[]{:S(2)}) %collective-permute-start.2) | collective-permute-done | bytes 481312 | tf_op jit(solution)/shard_map/ppermute | solution.py:22
  107.1 3.1 collective-permute-start.6
  110.2 6.4 %collective-permute-done.3 = bf16[32,7520]{1,0:T(8,128)(2,1)} collective-permute-done((bf16[32,7520]{1,0:T(8,128)(2,1)}, bf16[32,7520]{1,0:T(8,128)(2,1)}, u32[]{:S(2)}, u32[]{:S(2)}) %collective-permute-start.3) | collective-permute-done | bytes 481312 | tf_op jit(solution)/shard_map/ppermute | solution.py:22
  116.6 1.8 bitcast_dynamic-update-slice_fusion.7
  118.5 1.8 bitcast_dynamic-update-slice_fusion.6
  120.3 1.9 bitcast_dynamic-update-slice_fusion.5
  123.8 1.8 bitcast_dynamic-update-slice_fusion.2
  125.6 1.8 bitcast_dynamic-update-slice_fusion.1
  128.3 4.9 %gather_fusion = bf16[8,32,7520]{2,1,0:T(8,128)(2,1)} fusion(bf16[8,32,7520]{2,1,0:T(8,128)(2,1)} %bitcast_dynamic-update-slice_fusion, s32[1024]{0:T(1024)S(1)} %pad_clamp_fusion), kind=kCustom, calls=%fused_computation | custom fusion | bytes 7700512 | tf_op jit(solution)/shard_map/gather | solution.py:27
  137.8 6.1 %fusion.3 = f32[256,1024]{1,0:T(8,128)S(1)} fusion(bf16[1024,3696]{0,1:T(8,128)(2,1)} %param.11, bf16[256,7520]{1,0:T(8,128)(2,1)} %bitcast.45), kind=kOutput, calls=%fused_computation.8 | convolution fusion | flops 1937768448 | bytes 10518528 | tf_op jit(solution)/shard_map/dot_general | solution.py:32
  144.0 5.5 %fusion.7 = f32[256,1024]{1,0:T(8,128)S(1)} fusion(f32[256,1024]{1,0:T(8,128)S(1)} %fusion.3, bf16[1024,3696]{0,1:T(8,128)(2,1)} %param.10, bf16[256,7520]{1,0:T(8,128)(2,1)S(1)} %bitcast.46), kind=kOutput, calls=%fused_computation.13 | convolution fusion | flops 1938030592 | bytes 11567104 | tf_op jit(solution)/shard_map/dot_general | solution.py:32
  150.7 66.7 %all-reduce.3.cloned.1.call-done = bf16[1024,64]{0,1:T(8,128)(2,1)} async-done(((bf16[1024,64]{0,1:T(8,128)(2,1)}), bf16[1024,64]{0,1:T(8,128)(2,1)}) %all-reduce.3.cloned.1.call-update) | async-done | bytes 131088 | tf_op jit(solution)/shard_map/psum | solution.py:111
  219.0 47.6 %all-reduce.5.cloned.1.call-done = bf16[8,64,1024]{2,1,0:T(8,128)(2,1)} async-done(((bf16[8,64,1024]{2,1,0:T(8,128)(2,1)}), bf16[8,64,1024]{2,1,0:T(8,128)(2,1)}) %all-reduce.5.cloned.1.call-update) | async-done | bytes 1048592 | tf_op jit(solution)/shard_map/psum | solution.py:104
  266.6 2.8 convert_element_type.87
  269.4 73.1 %reduce-scatter.5.cloned.1.call-done = bf16[32,1024]{1,0:T(8,128)(2,1)} async-done(((bf16[256,1024]{1,0:T(8,128)(2,1)}), bf16[32,1024]{1,0:T(8,128)(2,1)}) %reduce-scatter.5.cloned.1.call-update) | async-done | bytes 65552 | tf_op jit(solution)/shard_map/reduce_scatter | solution.py:95
  (54 shorter events, 16.4 us)
Async XLA Ops:
  7.2 11.3 %copy-start = (bf16[8,64,1024]{2,1,0:T(8,128)(2,1)S(1)}, bf16[8,64,1024]{2,1,0:T(8,128)(2,1)}, u32[]{:S(2)}) copy-start(bf16[8,64,1024]{2,1,0:T(8,128)(2,1)} %param.14) | copy-start | bytes 3145732
  7.2 68.9 %reduce-scatter.7.cloned.1.call-start = ((), (), s32[]{:S(2)}) async-start(), calls=%async_computation.5 | async-start | bytes 6488064 | tf_op jit(solution)/shard_map/reduce_scatter | solution.py:65
  8.1 6.9 %copy-start.2 = (bf16[256,1024]{1,0:T(8,128)(2,1)S(1)}, bf16[256,1024]{1,0:T(8,128)(2,1)}, u32[]{:S(2)}) copy-start(bf16[256,1024]{1,0:T(8,128)(2,1)} %param.8) | copy-start | bytes 1572868
  8.1 6.9 %copy-start.6 = (bf16[1024,3696]{0,1:T(8,128)(2,1)S(1)}, bf16[1024,3696]{0,1:T(8,128)(2,1)}, u32[]{:S(2)}) copy-start(bf16[1024,3696]{0,1:T(8,128)(2,1)} %param.11) | copy-start | bytes 22708228
  8.1 10.9 %slice-start = ((s8[7569408]{0:T(1024)(128)(4,1)}), s8[4194304]{0:T(1024)(128)(4,1)S(1)}, s32[]{:S(2)}) async-start(s8[7569408]{0:T(1024)(128)(4,1)} %bitcast.51), calls=%async_computation.6 | async-start | bytes 8388608
  15.0 3.5 %copy-start.3 = (bf16[256,1024]{1,0:T(8,128)(2,1)S(1)}, bf16[256,1024]{1,0:T(8,128)(2,1)}, u32[]{:S(2)}) copy-start(bf16[256,1024]{1,0:T(8,128)(2,1)} %param.9) | copy-start | bytes 1572868
  15.0 4.0 %slice-start.1 = ((s8[7569408]{0:T(1024)(128)(4,1)}), s8[3375104]{0:T(1024)(128)(4,1)S(1)}, s32[]{:S(2)}) async-start(s8[7569408]{0:T(1024)(128)(4,1)} %bitcast.51), calls=%async_computation.7 | async-start | bytes 6750208
  19.0 3.4 copy-start.4
  32.4 185.1 %all-reduce.3.cloned.1.call-start = ((), (), s32[]{:S(2)}) async-start(), calls=%async_computation.3 | async-start | bytes 262144 | tf_op jit(solution)/shard_map/psum | solution.py:111
  78.7 9.4 %collective-permute-start = (bf16[32,7520]{1,0:T(8,128)(2,1)S(1)}, bf16[32,7520]{1,0:T(8,128)(2,1)S(1)}, u32[]{:S(2)}, u32[]{:S(2)}) collective-permute-start(bf16[32,7520]{1,0:T(8,128)(2,1)S(1)} %concatenate.7), channel_id=1, source_target_pairs={{0,1},{1,2},{2,3},{3,4},{4,5},{5,6},{6,7},{7,0},{8,9},{9,10},{10,1... | collective-permute-start | bytes 1443848 | tf_op jit(solution)/shard_map/ppermute | solution.py:22
  88.1 9.4 %collective-permute-start.1 = (bf16[32,7520]{1,0:T(8,128)(2,1)S(1)}, bf16[32,7520]{1,0:T(8,128)(2,1)S(1)}, u32[]{:S(2)}, u32[]{:S(2)}) collective-permute-start(bf16[32,7520]{1,0:T(8,128)(2,1)S(1)} %collective-permute-done), channel_id=1, source_target_pairs={{0,1},{1,2},{2,3},{3,4},{4,5},{5,6},{6,7},{7,0},{8,9},{9,10},{10,1... | collective-permute-start | bytes 1443848 | tf_op jit(solution)/shard_map/ppermute | solution.py:22
  88.1 9.4 %collective-permute-start.4 = (bf16[32,7520]{1,0:T(8,128)(2,1)S(1)}, bf16[32,7520]{1,0:T(8,128)(2,1)}, u32[]{:S(2)}, u32[]{:S(2)}) collective-permute-start(bf16[32,7520]{1,0:T(8,128)(2,1)S(1)} %concatenate.7), channel_id=1, source_target_pairs={{1,0},{2,1},{3,2},{4,3},{5,4},{6,5},{7,6},{0,7},{9,8},{10,9},{11,1... | collective-permute-start | bytes 1443848 | tf_op jit(solution)/shard_map/ppermute | solution.py:24
  97.4 0.8 copy-start.5
  97.5 9.5 %collective-permute-start.2 = (bf16[32,7520]{1,0:T(8,128)(2,1)S(1)}, bf16[32,7520]{1,0:T(8,128)(2,1)}, u32[]{:S(2)}, u32[]{:S(2)}) collective-permute-start(bf16[32,7520]{1,0:T(8,128)(2,1)S(1)} %collective-permute-done.1), channel_id=1, source_target_pairs={{0,1},{1,2},{2,3},{3,4},{4,5},{5,6},{6,7},{7,0},{8,9},{9,10},{10,1... | collective-permute-start | bytes 1443848 | tf_op jit(solution)/shard_map/ppermute | solution.py:22
  98.2 8.9 %collective-permute-start.5 = (bf16[32,7520]{1,0:T(8,128)(2,1)}, bf16[32,7520]{1,0:T(8,128)(2,1)}, u32[]{:S(2)}, u32[]{:S(2)}) collective-permute-start(bf16[32,7520]{1,0:T(8,128)(2,1)} %collective-permute-done.4), channel_id=1, source_target_pairs={{1,0},{2,1},{3,2},{4,3},{5,4},{6,5},{7,6},{0,7},{9,8},{10,9},{11,1... | collective-permute-start | bytes 1443848 | tf_op jit(solution)/shard_map/ppermute | solution.py:24
  106.9 9.7 %collective-permute-start.3 = (bf16[32,7520]{1,0:T(8,128)(2,1)}, bf16[32,7520]{1,0:T(8,128)(2,1)}, u32[]{:S(2)}, u32[]{:S(2)}) collective-permute-start(bf16[32,7520]{1,0:T(8,128)(2,1)} %collective-permute-done.2), channel_id=1, source_target_pairs={{0,1},{1,2},{2,3},{3,4},{4,5},{5,6},{6,7},{7,0},{8,9},{9,10},{10,1... | collective-permute-start | bytes 1443848 | tf_op jit(solution)/shard_map/ppermute | solution.py:22
  107.1 20.4 %collective-permute-start.6 = (bf16[32,7520]{1,0:T(8,128)(2,1)}, bf16[32,7520]{1,0:T(8,128)(2,1)S(1)}, u32[]{:S(2)}, u32[]{:S(2)}) collective-permute-start(bf16[32,7520]{1,0:T(8,128)(2,1)} %collective-permute-done.5), channel_id=1, source_target_pairs={{1,0},{2,1},{3,2},{4,3},{5,4},{6,5},{7,6},{0,7},{9,8},{10,9},{11,1... | collective-permute-start | bytes 1443848 | tf_op jit(solution)/shard_map/ppermute | solution.py:24
  136.1 130.6 %all-reduce.5.cloned.1.call-start = ((), (), s32[]{:S(2)}) async-start(), calls=%async_computation.4 | async-start | bytes 2097152 | tf_op jit(solution)/shard_map/psum | solution.py:104
  137.6 204.9 %reduce-scatter.5.cloned.1.call-start = ((), (), s32[]{:S(2)}) async-start(), calls=%async_computation.2 | async-start | bytes 589824 | tf_op jit(solution)/shard_map/reduce_scatter | solution.py:95
  137.8 6.1 %copy-start.1 = (bf16[8,32,7520]{2,1,0:T(8,128)(2,1)S(1)}, bf16[8,32,7520]{2,1,0:T(8,128)(2,1)}, u32[]{:S(2)}) copy-start(bf16[8,32,7520]{2,1,0:T(8,128)(2,1)} %gather_fusion) | copy-start | bytes 11550724
Sparse Core Ops, SparseCore 0:
  32.5 43.5 reduce-scatter.6
  136.2 81.1 all-reduce.2
  220.6 46.0 all-reduce.4
  270.6 71.8 reduce-scatter.4
